TPU v7x, 32 devices: a whole 2x2x4 slice. The times are simulated.
32 devices in a mesh: patch: 16 (over z, y, core), chan: 2 (over x).
Axes of the slice: x: 2, y: 2, z: 4, core: 2. Of those that a mesh axis runs over, the one named last changes fastest.
Arguments:
- fields: bfloat16 [16, 128, 1024], P('patch', 'chan'), may hold values from -6 to 6
- w_one: bfloat16 [9, 512, 128], P(None, 'chan'), may hold values from -0.1875 to 0.1875
- bias_one: float32 [512], P('chan'), may hold values from -3 to 3
- w_two: bfloat16 [9, 128, 512], P(None, None, 'chan'), may hold values from -0.09375 to 0.09375
- neighbour: int32 [16, 4], replicated, may hold values from 0 to 15, as said below
- seam_code: int32 [16, 4], replicated, may hold values from 0 to 7, as said below
- band_order: int32 [16], replicated, may hold values from 0 to 15, each once
- target: bfloat16 [16, 128, 1024], P('patch', 'chan'), may hold values from -6 to 6
- lat_weight: bfloat16 [16, 1024], P('patch'), may hold values from 0.099609375 to 1
Outputs:
- loss_value: float32 [], replicated
- grad_one: float32 [9, 512, 128], P(None, 'chan')
- grad_two: float32 [9, 128, 512], P(None, None, 'chan')
- grad_bias: float32 [512], P('chan')
Inputs may be any that keep to these rules, and one draw needn't show every extreme that they name: The sides of all patches are paired: side s of patch p borders side t = seam_code[p, s] mod 4 of patch q = neighbour[p, s], and then neighbour[q, t] = p, seam_code[q, t] mod 4 = s, and both codes agree on being 4 or more; so every edge is read by exactly one side of one other patch, and the four sides of a patch face four different patches. `seam_code`: code mod 4 names the neighbour's edge that forms the seam; codes 4 and above run that edge reversed, alike on both sides of a seam. `band_order`: each patch fills exactly one slot of every band.
All inputs are finite; a program needn't handle non-finite values.
Results may differ from a plain program's by a relative error of at most 0.0021.
Values may be sent and summed in bfloat16 or wider, within the bound.
A program may use at most 64 MiB of HBM per device.

v0:
```python
import math
import jax
import jax.numpy as jnp
from jax import lax
from jax.sharding import PartitionSpec as P

P_SIZE = 32


def edges_of(grid):
    return jnp.stack([grid[0], grid[-1], grid[:, 0], grid[:, -1]])


def with_frame(grid, strips):
    rows = jnp.concatenate([strips[0][None], grid, strips[1][None]], axis=0)
    left = jnp.pad(strips[2], ((1, 1), (0, 0)))[:, None]
    right = jnp.pad(strips[3], ((1, 1), (0, 0)))[:, None]
    return jnp.concatenate([left, rows, right], axis=1)


def conv(values, weight, pad, spec):
    return lax.conv_general_dilated(
        values[None],
        weight,
        (1, 1),
        ((pad, pad), (pad, pad)),
        dimension_numbers=("NHWC", spec, "NHWC"),
        preferred_element_type=jnp.float32,
    )[0]


def smooth_gate(values):
    return jax.nn.gelu(values, approximate=True)


def on_device(fields, w_one, bias_one, w_two, neighbour, seam_code, band_order, target, lat_weight):
    length = P_SIZE
    cells = length * length
    count = lax.axis_size("patch")
    chans = lax.axis_size("chan")
    part = cells // count
    own = lax.axis_index("patch")
    own_nbr = lax.dynamic_slice_in_dim(neighbour, own, 1, 0)[0]
    own_code = lax.dynamic_slice_in_dim(seam_code, own, 1, 0)[0]
    ids = jnp.arange(count, dtype=jnp.int32)
    faces = (own_nbr[:, None] == ids[None, :]).astype(jnp.bfloat16)
    turned = (own_code >= 4)[:, None, None]
    inner = w_one.shape[1]

    def to_send(grid):
        strips = edges_of(grid)
        strips = jnp.where(turned, strips[:, ::-1], strips)
        return jnp.einsum("tr,tkc->rkc", faces, strips, preferred_element_type=jnp.float32).astype(
            jnp.bfloat16
        )

    def picked(arrived):
        return jnp.einsum("tr,rkc->tkc", faces, arrived, preferred_element_type=jnp.float32).astype(
            jnp.bfloat16
        )

    def swap(sent):
        return lax.all_to_all(sent, "patch", split_axis=0, concat_axis=0, tiled=True)

    both = lax.all_gather(jnp.stack([fields[0], target[0]]), "chan", axis=1, tiled=True)
    chan_full = both.shape[1]
    x_grid = both[0].T.reshape(length, length, chan_full)
    slots = (band_order[None, :] == ids[:, None]).astype(jnp.bfloat16)
    lat_rows = -(-part // chan_full)
    lat_parts = jnp.pad(
        lat_weight.reshape(count, part), ((0, 0), (0, lat_rows * chan_full - part))
    ).reshape(count, lat_rows, chan_full)
    band_parts = jnp.concatenate([both[1].T.reshape(count, part, chan_full), lat_parts], axis=1)
    band_parts = jnp.einsum(
        "ps,skc->pkc", slots, band_parts, preferred_element_type=jnp.float32
    ).astype(jnp.bfloat16)
    first = swap(jnp.concatenate([to_send(x_grid), band_parts], axis=1))
    x_pad = with_frame(x_grid, picked(first[:, :length]))
    target_patch = first[:, length : length + part].reshape(cells, chan_full)
    lat_w = (
        first[:, length + part :]
        .reshape(count, lat_rows * chan_full)[:, :part]
        .reshape(cells, 1)
        .astype(jnp.float32)
    )
    preact = conv(x_pad, w_one.reshape(3, 3, inner, chan_full), 0, "HWOI") + bias_one
    hidden = smooth_gate(preact).astype(jnp.bfloat16)
    h_pad = with_frame(hidden, picked(swap(to_send(hidden))))
    partial = conv(h_pad, w_two.reshape(3, 3, chan_full, inner), 0, "HWOI").reshape(
        cells, chan_full
    )
    mixed = partial
    rounded = partial.astype(jnp.bfloat16)
    for shift in range(1, chans):
        mixed = mixed + lax.ppermute(
            rounded, "chan", [(i, (i + shift) % chans) for i in range(chans)]
        ).astype(jnp.float32)
    x_flat = x_grid.reshape(cells, chan_full)
    misfit = x_flat.astype(jnp.float32) + mixed - target_patch.astype(jnp.float32)
    weighted = lat_w * misfit
    loss_local = jnp.sum(weighted * misfit)
    inv_root = 1.0 / math.sqrt(count * cells)
    grad_out = (weighted * inv_root).astype(jnp.bfloat16)
    g_grid = grad_out.reshape(length, length, chan_full)
    h_taps = [
        h_pad[a : a + length, b : b + length].reshape(cells, inner)
        for a in range(3)
        for b in range(3)
    ]
    two_local = jnp.stack(
        [
            lax.dot_general(
                grad_out, tap, (((0,), (0,)), ((), ())), preferred_element_type=jnp.float32
            )
            for tap in h_taps
        ]
    )
    near = picked(swap(to_send(g_grid)))
    side_taps = jnp.array([[0, 1, 2], [6, 7, 8], [0, 3, 6], [2, 5, 8]], jnp.int32)
    used = side_taps[own_code % 4]
    used = jnp.where((own_code >= 4)[:, None], used[:, ::-1], used)
    hot = (used[:, :, None] == jnp.arange(9)[None, None, :]).astype(jnp.bfloat16)
    spread = jnp.pad(near, ((0, 0), (1, 1), (0, 0)))
    shifted = jnp.stack([spread[:, 2 - d : 2 - d + length] for d in range(3)], axis=1)
    side_in = jnp.einsum("tdn,tdkc->tknc", hot, shifted, preferred_element_type=jnp.float32).astype(
        jnp.bfloat16
    )
    back = lax.dot_general(
        side_in.reshape(4 * length, 9 * chan_full),
        w_two.reshape(9 * chan_full, inner),
        (((1,), (0,)), ((), ())),
        preferred_element_type=jnp.float32,
    ).reshape(4, length, inner)
    grad_h = conv(g_grid, w_two.reshape(3, 3, chan_full, inner)[::-1, ::-1], 1, "HWIO")
    row = lax.broadcasted_iota(jnp.int32, (length, length, 1), 0)
    col = lax.broadcasted_iota(jnp.int32, (length, length, 1), 1)
    grad_h = (
        grad_h
        + jnp.where(row == 0, back[0][None], 0.0)
        + jnp.where(row == length - 1, back[1][None], 0.0)
        + jnp.where(col == 0, back[2][:, None], 0.0)
        + jnp.where(col == length - 1, back[3][:, None], 0.0)
    )
    grad_pre = jax.vjp(smooth_gate, preact)[1](grad_h)[0].reshape(cells, inner)
    bias_local = jnp.sum(grad_pre, axis=0)
    pre_b = grad_pre.astype(jnp.bfloat16)
    x_taps = [
        x_pad[a : a + length, b : b + length].reshape(cells, chan_full)
        for a in range(3)
        for b in range(3)
    ]
    one_local = jnp.stack(
        [
            lax.dot_general(
                pre_b, tap, (((0,), (0,)), ((), ())), preferred_element_type=jnp.float32
            )
            for tap in x_taps
        ]
    )
    small_rows = -(-inner // chan_full) + 1
    small = jnp.concatenate(
        [
            jnp.pad(bias_local, (0, (small_rows - 1) * chan_full - inner)),
            jnp.pad(loss_local[None], (0, chan_full - 1)),
        ]
    ).reshape(small_rows, chan_full)
    sum_two = lax.psum(two_local, "patch")
    sums = lax.psum(
        jnp.concatenate([one_local.reshape(9 * inner, chan_full), small], axis=0), "patch"
    )
    grad_one = sums[: 9 * inner].reshape(9, inner, chan_full)
    grad_bias = sums[9 * inner : -1].reshape(-1)[:inner]
    loss_value = sums[-1, 0] / (count * cells * chan_full)
    return (loss_value, grad_one, sum_two, grad_bias)


def solution(mesh):
    placed = (
        P("patch", "chan", None),
        P(None, "chan", None),
        P("chan"),
        P(None, None, "chan"),
        P(),
        P(),
        P(),
        P("patch", "chan", None),
        P("patch", None),
    )
    return jax.shard_map(
        on_device,
        mesh=mesh,
        in_specs=placed,
        out_specs=(P(), P(None, "chan", None), P(None, None, "chan"), P("chan")),
        check_vma=False,
    )
```

profile of v0, /device:TPU:0, one launch (start us, length us, event | category | flops | bytes accessed | tf_op | source)
XLA Modules:
  0.0 233.3 jit_solution(5168928998311883322)
XLA Ops:
  7.2 1.2 copy.213
  8.4 1.1 copy.214
  10.1 9.9 %all_gather.3 = bf16[2,128,1024]{2,0,1:T(2,128)(2,1)S(1)} all-gather(bf16[2,64,1024]{2,0,1:T(2,128)(2,1)S(1)} %pad_maximum_fusion.8), channel_id=1, replica_groups=mesh['patch'=16,'chan'=2] {'chan'}, dimensions={1}, use_global_device_ids=true | all-gather | bytes 786432 | tf_op jit(solution)/shard_map/all_gather | solution.py:65
  23.2 0.9 copy.219
  24.0 6.2 %all-to-all-start = ((bf16[16,97,128]{2,1,0:T(8,128)(2,1)}), bf16[16,97,128]{2,1,0:T(8,128)(2,1)S(1)}, u32[]{:S(2)}, u32[]{:S(2)}) async-start(bf16[16,97,128]{2,1,0:T(8,128)(2,1)} %copy.219), calls=%async_computation | async-start | bytes 851968 | tf_op jit(solution)/shard_map/all_to_all | solution.py:63
  32.2 10.8 %all-to-all-done = bf16[16,97,128]{2,1,0:T(8,128)(2,1)S(1)} async-done(((bf16[16,97,128]{2,1,0:T(8,128)(2,1)}), bf16[16,97,128]{2,1,0:T(8,128)(2,1)S(1)}, u32[]{:S(2)}, u32[]{:S(2)}) %all-to-all-start) | async-done | bytes 397344 | tf_op jit(solution)/shard_map/all_to_all | solution.py:63
  44.3 2.3 subtract_multiply_fusion
  47.5 1.0 slice.267
  48.5 1.4 add_multiply_fusion
  50.0 1.5 copy.250
  51.7 0.9 pad_maximum_fusion.6
  54.7 4.4 %all-to-all-start.1 = ((bf16[16,32,256]{2,1,0:T(8,128)(2,1)}), bf16[16,32,256]{2,1,0:T(8,128)(2,1)}, u32[]{:S(2)}, u32[]{:S(2)}) async-start(bf16[16,32,256]{2,1,0:T(8,128)(2,1)} %copy.233), calls=%async_computation.1 | async-start | bytes 524288 | tf_op jit(solution)/shard_map/all_to_all | solution.py:63
  59.9 1.9 copy.262
  61.9 1.5 copy.249
  63.4 1.5 copy.252
  64.8 1.5 copy.251
  66.3 1.0 fusion.123
  67.3 1.0 fusion.122
  68.3 1.1 fusion.38
  69.4 1.2 convolution_convert_fusion.5
  73.2 0.8 copy-done.19
  74.0 1.7 convolution_select_fusion.2
  76.2 1.6 collective-permute-start
  78.5 1.1 copy.260
  79.5 1.1 copy.261
  81.6 1.1 copy.266
  82.7 1.9 collective-permute-done
  85.4 0.9 fusion.13
  86.7 1.0 convolution_select_fusion
  87.7 1.7 copy.242
  90.6 5.9 %all-to-all-start.2 = ((bf16[16,32,128]{2,1,0:T(8,128)(2,1)}), bf16[16,32,128]{2,1,0:T(8,128)(2,1)}, u32[]{:S(2)}, u32[]{:S(2)}) async-start(bf16[16,32,128]{2,1,0:T(8,128)(2,1)} %copy.246), calls=%async_computation.2 | async-start | bytes 262144 | tf_op jit(solution)/shard_map/all_to_all | solution.py:63
  96.5 0.9 fusion.12
  97.5 2.0 fusion.11
  99.4 0.9 fusion.10
  100.4 0.9 fusion.9
  101.3 0.9 fusion.8
  102.2 0.9 fusion.7
  103.1 0.9 fusion.6
  104.1 0.9 fusion.5
  105.0 1.2 convolution_convert_fusion.6
  106.8 1.3 fusion.74
  108.2 3.8 %fusion.116 = (bf16[1,32,32,256]{3,1,2,0:T(8,128)(2,1)S(1)}, f32[1,32,32,256]{3,1,2,0:T(8,128)}) fusion(f32[32,1,40,256]{3,0,2,1:T(8,128)} %bitcast.352, f32[32,1,40,256]{3,0,2,1:T(8,128)} %bitcast.353, f32[32,1,40,256]{3,0,2,1:T(8,128)S(1)} %bitcast.350, f32[32,1,40,256]{3,0,2,1:T(8,128)S(1)} %bitcast.351, f32[32,256]{1,0:T(8,128)S(1)} %get-tuple-element.49, ...), kind=kLoop, calls=%fused_computation.217 | loop fusion | flops 4718592 | bytes 6948864 | tf_op jit(solution)/shard_map/convert_element_type | solution.py:146
  116.8 1.1 pad_maximum_fusion
  117.9 100.8 %all-reduce.10.cloned.1.call-done = (f32[2307,128]{1,0:T(8,128)}, f32[9,128,256]{2,1,0:T(8,128)}) async-done(((f32[2307,128]{1,0:T(8,128)}, f32[9,128,256]{2,1,0:T(8,128)}), (f32[2307,128]{1,0:T(8,128)}, f32[9,128,256]{2,1,0:T(8,128)})) %all-reduce.10.cloned.1.call-update) | async-done | bytes 2360848 | tf_op jit(solution)/shard_map/psum | solution.py:168
  218.8 2.5 %slice.300 = f32[2304,128]{1,0:T(8,128)} slice(f32[2307,128]{1,0:T(8,128)} %get-tuple-element.4), slice={[0:2304], [0:128]} | slice | bytes 2359296 | tf_op jit(solution)/shard_map/slice | solution.py:171
  221.2 1.2 slice.299
  222.4 1.2 slice_bitcast_fusion.13
  224.3 1.0 copy.337
  (182 shorter events, 22.7 us)
Async XLA Ops:
  7.2 36.7 %copy-start = (bf16[9,256,128]{2,1,0:T(8,128)(2,1)S(1)}, bf16[9,256,128]{2,1,0:T(8,128)(2,1)}, u32[]{:S(2)}) copy-start(bf16[9,256,128]{2,1,0:T(8,128)(2,1)} %param.11) | copy-start | bytes 1769476
  20.0 1.3 copy-start.24
  20.0 1.5 copy-start.30
  20.7 1.7 copy-start.25
  20.7 2.2 copy-start.31
  23.1 7.2 %copy-start.22 = (s32[4,3]{1,0:T(4,128)S(1)}, s32[4,3]{1,0:T(4,128)}, u32[]{:S(2)}) copy-start(s32[4,3]{1,0:T(4,128)} %constant.54.clone) | copy-start | bytes 148
  24.0 18.9 %all-to-all-start = ((bf16[16,97,128]{2,1,0:T(8,128)(2,1)}), bf16[16,97,128]{2,1,0:T(8,128)(2,1)S(1)}, u32[]{:S(2)}, u32[]{:S(2)}) async-start(bf16[16,97,128]{2,1,0:T(8,128)(2,1)} %copy.219), calls=%async_computation | async-start | bytes 851968 | tf_op jit(solution)/shard_map/all_to_all | solution.py:63
  43.0 0.8 copy-start.8
  43.6 0.7 copy-start.26
  43.6 0.7 copy-start.32
  47.5 5.1 %copy-start.20 = (bf16[1,32,256]{2,1,0:T(8,128)(2,1)}, bf16[1,32,256]{2,1,0:T(8,128)(2,1)S(1)}, u32[]{:S(2)}) copy-start(bf16[1,32,256]{2,1,0:T(8,128)(2,1)S(1)} %get-tuple-element.26) | copy-start | bytes 49156
  47.5 5.1 %copy-start.21 = (bf16[1,32,256]{2,1,0:T(8,128)(2,1)}, bf16[1,32,256]{2,1,0:T(8,128)(2,1)S(1)}, u32[]{:S(2)}) copy-start(bf16[1,32,256]{2,1,0:T(8,128)(2,1)S(1)} %get-tuple-element.27) | copy-start | bytes 49156
  54.7 14.8 %all-to-all-start.1 = ((bf16[16,32,256]{2,1,0:T(8,128)(2,1)}), bf16[16,32,256]{2,1,0:T(8,128)(2,1)}, u32[]{:S(2)}, u32[]{:S(2)}) async-start(bf16[16,32,256]{2,1,0:T(8,128)(2,1)} %copy.233), calls=%async_computation.1 | async-start | bytes 524288 | tf_op jit(solution)/shard_map/all_to_all | solution.py:63
  59.9 1.9 copy-start.1
  63.4 1.5 copy-start.9
  67.3 1.0 copy-start.27
  72.9 1.1 copy-start.19
  72.9 1.1 copy-start.33
  76.2 8.3 %collective-permute-start = (bf16[1024,128]{1,0:T(8,128)(2,1)S(1)}, bf16[1024,128]{1,0:T(8,128)(2,1)S(1)}, u32[]{:S(2)}, u32[]{:S(2)}) collective-permute-start(bf16[1024,128]{1,0:T(8,128)(2,1)S(1)} %bitcast_convert_fusion), channel_id=1, source_target_pairs={{0,1},{1,0},{2,3},{3,2},{4,5},{5,4},{6,7},{7,6},{8,9},{9,8},{10,11... | collective-permute-start | bytes 786440 | tf_op jit(solution)/shard_map/ppermute | solution.py:95
  81.3 3.3 %slice-start = ((bf16[16,97,128]{2,1,0:T(8,128)(2,1)}), bf16[16,64,128]{2,1,0:T(8,128)(2,1)S(1)}, s32[]{:S(2)}) async-start(bf16[16,97,128]{2,1,0:T(8,128)(2,1)} %copy-done.8), calls=%async_computation.4 | async-start | bytes 524288 | tf_op jit(solution)/shard_map/slice | solution.py:79
  90.6 14.4 %all-to-all-start.2 = ((bf16[16,32,128]{2,1,0:T(8,128)(2,1)}), bf16[16,32,128]{2,1,0:T(8,128)(2,1)}, u32[]{:S(2)}, u32[]{:S(2)}) async-start(bf16[16,32,128]{2,1,0:T(8,128)(2,1)} %copy.246), calls=%async_computation.2 | async-start | bytes 262144 | tf_op jit(solution)/shard_map/all_to_all | solution.py:63
  96.4 122.3 %all-reduce.10.cloned.1.call-start = ((), (), s32[]{:S(2)}) async-start(), calls=%async_computation.3 | async-start | bytes 4726784 | tf_op jit(solution)/shard_map/psum | solution.py:168
  96.5 2.9 %copy-start.6 = (bf16[32,32,256]{2,1,0:T(8,128)(2,1)S(1)}, bf16[32,32,256]{2,1,0:T(8,128)(2,1)}, u32[]{:S(2)}) copy-start(bf16[32,32,256]{2,1,0:T(8,128)(2,1)} %copy.261) | copy-start | bytes 1572868
  96.5 3.8 %copy-start.7 = (bf16[1024,256]{1,0:T(8,128)(2,1)S(1)}, bf16[1024,256]{1,0:T(8,128)(2,1)}, u32[]{:S(2)}) copy-start(bf16[1024,256]{1,0:T(8,128)(2,1)} %fusion.38) | copy-start | bytes 1572868
  101.3 2.8 %copy-start.5 = (bf16[32,32,256]{2,1,0:T(8,128)(2,1)S(1)}, bf16[32,32,256]{2,1,0:T(8,128)(2,1)}, u32[]{:S(2)}) copy-start(bf16[32,32,256]{2,1,0:T(8,128)(2,1)} %copy.266) | copy-start | bytes 1572868
  103.1 3.2 %copy-start.23 = (s32[4,3]{1,0:T(4,128)S(1)}, s32[4,3]{1,0:T(4,128)}, u32[]{:S(2)}) copy-start(s32[4,3]{1,0:T(4,128)} %broadcast_select_fusion.3) | copy-start | bytes 148
  104.1 4.1 %copy-start.3 = (f32[32,8,5,256]{3,0,2,1:T(8,128)S(1)}, f32[32,8,5,256]{3,0,2,1:T(8,128)}, u32[]{:S(2)}) copy-start(f32[32,8,5,256]{3,0,2,1:T(8,128)} %copy.249) | copy-start | bytes 3932164
  105.0 3.1 %copy-start.2 = (f32[32,8,5,256]{3,0,2,1:T(8,128)S(1)}, f32[32,8,5,256]{3,0,2,1:T(8,128)}, u32[]{:S(2)}) copy-start(f32[32,8,5,256]{3,0,2,1:T(8,128)} %copy.250) | copy-start | bytes 3932164
  105.0 3.1 %copy-start.28 = (pred[32]{0:T(512)(128)(4,1)S(1)}, pred[32]{0:T(512)(128)(4,1)}, u32[]{:S(2)}) copy-start(pred[32]{0:T(512)(128)(4,1)} %get-tuple-element.67) | copy-start | bytes 100
  105.0 3.2 %copy-start.29 = (pred[32]{0:T(512)(128)(4,1)S(1)}, pred[32]{0:T(512)(128)(4,1)}, u32[]{:S(2)}) copy-start(pred[32]{0:T(512)(128)(4,1)} %get-tuple-element.68) | copy-start | bytes 100
  108.2 4.1 %copy-start.17 = (bf16[32,32,128]{2,1,0:T(8,128)(2,1)S(1)}, bf16[32,32,128]{2,1,0:T(8,128)(2,1)}, u32[]{:S(2)}) copy-start(bf16[32,32,128]{2,1,0:T(8,128)(2,1)} %get-tuple-element.35) | copy-start | bytes 786436
  111.9 0.9 copy-start.12
  112.0 1.3 copy-start.18
  112.3 1.3 copy-start.15
  113.3 1.1 copy-start.16
  113.6 1.1 copy-start.13
  114.0 1.1 copy-start.11
  114.3 1.1 copy-start.14
  114.7 1.3 copy-start.4
  218.8 5.5 %copy-start.10 = (f32[9,128,256]{2,1,0:T(8,128)S(1)}, f32[9,128,256]{2,1,0:T(8,128)}, u32[]{:S(2)}) copy-start(f32[9,128,256]{2,1,0:T(8,128)} %get-tuple-element.71) | copy-start | bytes 3538948
Sparse Core Ops, SparseCore 0:
  118.0 100.6 all-reduce.9
where the time goes:
time: 234 us; the launch traced here: 233 us
  waiting for transfers between devices  114 us (49%)
  local copies, waits for them, and re-layouts  36.7 us (16%)
  matrix products  23.1 us (10%)
  starting transfers between devices  18 us (8%)
  between operations  16.8 us (7%)
  other arithmetic  15.3 us (7%)
  blocking collectives  9.91 us (4%)
    psum x1, waiting for transfers between devices, on_device(): lax.psum(jnp.concatenate([one_local.reshape(9 * inner, chan_full), small]...  101 us
    all_to_all x3, starting transfers between devices, swap(): lax.all_to_all(sent, 'patch', split_axis=0, concat_axis=0, tiled=True)  16.4 us
    all_to_all x3, waiting for transfers between devices, swap(): lax.all_to_all(sent, 'patch', split_axis=0, concat_axis=0, tiled=True)  10.8 us
    all_gather x1, blocking collectives, on_device(): lax.all_gather(jnp.stack([fields[0], target[0]]), 'chan', axis=1, tiled=T...  9.91 us
    dot_general x9, matrix products, on_device(): lax.dot_general(grad_out, tap, (((0,), (0,)), ((), ())), preferred_elemen...  9.39 us
    unnamed x85, local copies, waits for them, and re-layouts  6.32 us
    conv_general_dilated x13, local copies, waits for them, and re-layouts, conv(): lax.conv_general_dilated(values[None], weight, (1, 1), ((pad, pad), (pad,...  6.06 us
    slice x10, local copies, waits for them, and re-layouts, on_device(): h_pad[a:a + length, b:b + length].reshape(cells, inner)  5.55 us
  transfers between devices with their start and end apart: 5, of which 3 were waited for; matrix products, arithmetic and copies ran while one was open for 11% of the time, Pallas kernels for 0%

commit v1 on v0

--- a/solution.py
+++ b/solution.py
@@ -165,8 +165,11 @@
         ]
     ).reshape(small_rows, chan_full)
     sum_two = lax.psum(two_local, "patch")
-    sums = lax.psum(
-        jnp.concatenate([one_local.reshape(9 * inner, chan_full), small], axis=0), "patch"
+    sums = jnp.sum(
+        lax.all_gather(
+            jnp.concatenate([one_local.reshape(9 * inner, chan_full), small], axis=0), "patch"
+        ),
+        axis=0,
     )
     grad_one = sums[: 9 * inner].reshape(9, inner, chan_full)
     grad_bias = sums[9 * inner : -1].reshape(-1)[:inner]

time: 234 us -> 318 us (1.36)
  waiting for transfers between devices: 114 us -> 189 us
  other arithmetic: 15.3 us -> 25.5 us
    all_gather x0 -> x1, waiting for transfers between devices: none -> 81.8 us  [on_device(): lax.all_gather(jnp.concatenate([one_local.reshape(9 * inner, chan_full),...]
    psum x1, waiting for transfers between devices: 101 us -> 87.5 us  [on_device(): sum_two = lax.psum(two_local, 'patch')]
    all_to_all x3, waiting for transfers between devices: 10.8 us -> 20 us  [swap(): lax.all_to_all(sent, 'patch', split_axis=0, concat_axis=0, tiled=True)]
    reduce_sum x0 -> x1, other arithmetic: none -> 7.38 us  [on_device(): jnp.sum(lax.all_gather(jnp.concatenate([one_local.reshape(9 * inner, chan...]
    unnamed x85 -> x111, local copies, waits for them, and re-layouts: 6.32 us -> 11 us
  transfers between devices with their start and end apart: 5 -> 6, of which waited for: 3 -> 5; matrix products, arithmetic and copies ran while one was open for 11% -> 13% of each run, Pallas kernels for 0% -> 0%
where the time goes in v1:
time: 318 us; the launch traced here: 317 us
  waiting for transfers between devices  189 us (59%)
  local copies, waits for them, and re-layouts  37.2 us (12%)
  other arithmetic  25.5 us (8%)
  matrix products  21.6 us (7%)
  between operations  16.9 us (5%)
  starting transfers between devices  16.1 us (5%)
  blocking collectives  9.91 us (3%)
    psum x1, waiting for transfers between devices, on_device(): sum_two = lax.psum(two_local, 'patch')  87.5 us
    all_gather x1, waiting for transfers between devices, on_device(): lax.all_gather(jnp.concatenate([one_local.reshape(9 * inner, chan_full),...  81.8 us
    all_to_all x3, waiting for transfers between devices, swap(): lax.all_to_all(sent, 'patch', split_axis=0, concat_axis=0, tiled=True)  20 us
    all_to_all x3, starting transfers between devices, swap(): lax.all_to_all(sent, 'patch', split_axis=0, concat_axis=0, tiled=True)  14.1 us
    unnamed x111, local copies, waits for them, and re-layouts  11 us
    all_gather x1, blocking collectives, on_device(): lax.all_gather(jnp.stack([fields[0], target[0]]), 'chan', axis=1, tiled=T...  9.91 us
    dot_general x9, matrix products, on_device(): lax.dot_general(grad_out, tap, (((0,), (0,)), ((), ())), preferred_elemen...  8.39 us
    reduce_sum x1, other arithmetic, on_device(): jnp.sum(lax.all_gather(jnp.concatenate([one_local.reshape(9 * inner, chan...  7.38 us
  transfers between devices with their start and end apart: 6, of which 5 were waited for; matrix products, arithmetic and copies ran while one was open for 13% of the time, Pallas kernels for 0%

profile of v1, /device:TPU:0, one launch (start us, length us, event | category | flops | bytes accessed | tf_op | source)
XLA Modules:
  0.0 316.6 jit_solution(12755892531535980469)
XLA Ops:
  7.2 1.2 copy.213
  8.4 1.1 copy.214
  10.1 9.9 %all_gather.9 = bf16[2,128,1024]{2,0,1:T(2,128)(2,1)S(1)} all-gather(bf16[2,64,1024]{2,0,1:T(2,128)(2,1)S(1)} %pad_maximum_fusion.7), channel_id=1, replica_groups=mesh['patch'=16,'chan'=2] {'chan'}, dimensions={1}, use_global_device_ids=true | all-gather | bytes 786432 | tf_op jit(solution)/shard_map/all_gather | solution.py:65
  23.2 0.9 copy.219
  24.1 6.2 %all-to-all-start = ((bf16[16,97,128]{2,1,0:T(8,128)(2,1)}), bf16[16,97,128]{2,1,0:T(8,128)(2,1)S(1)}, u32[]{:S(2)}, u32[]{:S(2)}) async-start(bf16[16,97,128]{2,1,0:T(8,128)(2,1)} %copy.219), calls=%async_computation | async-start | bytes 851968 | tf_op jit(solution)/shard_map/all_to_all | solution.py:63
  32.2 10.8 %all-to-all-done = bf16[16,97,128]{2,1,0:T(8,128)(2,1)S(1)} async-done(((bf16[16,97,128]{2,1,0:T(8,128)(2,1)}), bf16[16,97,128]{2,1,0:T(8,128)(2,1)S(1)}, u32[]{:S(2)}, u32[]{:S(2)}) %all-to-all-start) | async-done | bytes 397344 | tf_op jit(solution)/shard_map/all_to_all | solution.py:63
  44.4 2.4 subtract_multiply_fusion
  47.7 1.1 pad_maximum_fusion.4
  49.5 0.8 broadcast_select_fusion
  50.4 1.0 convolution_convert_fusion.2
  51.4 0.8 copy.233
  52.2 4.4 %all-to-all-start.1 = ((bf16[16,32,256]{2,1,0:T(8,128)(2,1)}), bf16[16,32,256]{2,1,0:T(8,128)(2,1)}, u32[]{:S(2)}, u32[]{:S(2)}) async-start(bf16[16,32,256]{2,1,0:T(8,128)(2,1)} %copy.233), calls=%async_computation.1 | async-start | bytes 524288 | tf_op jit(solution)/shard_map/all_to_all | solution.py:63
  57.3 2.2 fusion.123
  59.5 1.9 add_multiply_fusion
  61.4 5.1 %all-to-all-done.1 = bf16[16,32,256]{2,1,0:T(8,128)(2,1)} async-done(((bf16[16,32,256]{2,1,0:T(8,128)(2,1)}), bf16[16,32,256]{2,1,0:T(8,128)(2,1)}, u32[]{:S(2)}, u32[]{:S(2)}) %all-to-all-start.1) | async-done | bytes 262176 | tf_op jit(solution)/shard_map/all_to_all | solution.py:63
  66.4 1.2 convolution_convert_fusion.5
  68.6 0.8 copy-done.18
  69.5 1.7 convolution_select_fusion.2
  71.7 0.8 copy-done.3
  73.3 1.5 collective-permute-start
  74.8 0.9 pad_maximum_fusion.5
  75.7 1.5 copy.250
  77.2 2.9 copy.249
  80.1 1.5 copy.252
  81.6 1.5 copy.251
  83.1 1.0 fusion.122
  84.5 1.8 fusion.58
  88.5 3.5 %all-to-all-start.2 = ((bf16[16,32,128]{2,1,0:T(8,128)(2,1)}), bf16[16,32,128]{2,1,0:T(8,128)(2,1)S(1)}, u32[]{:S(2)}, u32[]{:S(2)}) async-start(bf16[16,32,128]{2,1,0:T(8,128)(2,1)} %copy.246), calls=%async_computation.2 | async-start | bytes 262144 | tf_op jit(solution)/shard_map/all_to_all | solution.py:63
  92.3 1.9 convolution_select_fusion
  94.2 1.5 copy.242
  95.7 4.2 %all-to-all-done.2 = bf16[16,32,128]{2,1,0:T(8,128)(2,1)S(1)} async-done(((bf16[16,32,128]{2,1,0:T(8,128)(2,1)}), bf16[16,32,128]{2,1,0:T(8,128)(2,1)S(1)}, u32[]{:S(2)}, u32[]{:S(2)}) %all-to-all-start.2) | async-done | bytes 131104 | tf_op jit(solution)/shard_map/all_to_all | solution.py:63
  101.2 3.1 fusion.116
  108.1 1.0 copy-done.8
  110.0 2.4 maximum_bitcast_fusion
  118.3 0.9 fusion.13
  119.2 0.9 fusion.12
  120.2 0.9 fusion.11
  121.1 0.9 fusion.10
  122.0 0.9 fusion.9
  123.0 0.9 fusion.8
  123.9 0.9 fusion.7
  124.8 0.9 fusion.6
  125.8 0.9 fusion.5
  126.7 81.8 %all-gather.4.cloned.1.call-done = f32[16,2307,128]{2,1,0:T(8,128)} async-done(((f32[1,2307,128]{2,1,0:T(8,128)}), f32[16,2307,128]{2,1,0:T(8,128)}) %all-gather.4.cloned.1.call-update) | async-done | bytes 18898960 | tf_op jit(solution)/shard_map/all_gather | solution.py:169
  208.5 7.4 %reduce_sum.29 = f32[2307,128]{1,0:T(8,128)S(1)} reduce(f32[16,2307,128]{2,1,0:T(8,128)} %all-gather.4.cloned.1.call-done, f32[]{:T(128)} %constant.49.clone.1), dimensions={0}, to_apply=%region_2.3 | reduce | flops 4429440 | bytes 20080132 | tf_op jit(solution)/shard_map/reduce_sum | solution.py:168
  215.9 1.1 slice.300
  218.7 87.5 %all-reduce.9.cloned.1.call-done = f32[9,128,256]{2,1,0:T(8,128)} async-done(((f32[9,128,256]{2,1,0:T(8,128)}), f32[9,128,256]{2,1,0:T(8,128)}) %all-reduce.9.cloned.1.call-update) | async-done | bytes 1179664 | tf_op jit(solution)/shard_map/psum | solution.py:167
  306.2 2.4 copy.336
  (212 shorter events, 26.9 us)
Async XLA Ops:
  7.2 36.8 %copy-start = (bf16[9,256,128]{2,1,0:T(8,128)(2,1)S(1)}, bf16[9,256,128]{2,1,0:T(8,128)(2,1)}, u32[]{:S(2)}) copy-start(bf16[9,256,128]{2,1,0:T(8,128)(2,1)} %param.11) | copy-start | bytes 1769476
  20.0 1.3 copy-start.37
  20.0 1.5 copy-start.43
  20.7 1.7 copy-start.38
  20.7 2.2 copy-start.44
  21.5 10.0 %copy-start.34 = (pred[4]{0:T(512)(128)(4,1)}, pred[4]{0:T(512)(128)(4,1)S(1)}, u32[]{:S(2)}) copy-start(pred[4]{0:T(512)(128)(4,1)S(1)} %compare_reduce_fusion) | copy-start | bytes 16
  21.7 21.3 %copy-start.32 = (s32[4]{0:T(128)}, s32[4]{0:T(128)S(1)}, u32[]{:S(2)}) copy-start(s32[4]{0:T(128)S(1)} %get-tuple-element.63) | copy-start | bytes 52
  23.1 7.2 %copy-start.31 = (s32[4,3]{1,0:T(4,128)S(1)}, s32[4,3]{1,0:T(4,128)}, u32[]{:S(2)}) copy-start(s32[4,3]{1,0:T(4,128)} %constant.54.clone) | copy-start | bytes 148
  24.1 18.9 %all-to-all-start = ((bf16[16,97,128]{2,1,0:T(8,128)(2,1)}), bf16[16,97,128]{2,1,0:T(8,128)(2,1)S(1)}, u32[]{:S(2)}, u32[]{:S(2)}) async-start(bf16[16,97,128]{2,1,0:T(8,128)(2,1)} %copy.219), calls=%async_computation | async-start | bytes 851968 | tf_op jit(solution)/shard_map/all_to_all | solution.py:63
  43.0 0.8 copy-start.7
  43.3 4.4 %copy-start.27 = (bf16[1,32,128]{2,1,0:T(8,128)(2,1)}, bf16[1,32,128]{2,1,0:T(8,128)(2,1)S(1)}, u32[]{:S(2)}) copy-start(bf16[1,32,128]{2,1,0:T(8,128)(2,1)S(1)} %copy.222) | copy-start | bytes 24580
  43.3 4.4 %copy-start.29 = (bf16[1,32,128]{2,1,0:T(8,128)(2,1)}, bf16[1,32,128]{2,1,0:T(8,128)(2,1)S(1)}, u32[]{:S(2)}) copy-start(bf16[1,32,128]{2,1,0:T(8,128)(2,1)S(1)} %copy.223) | copy-start | bytes 24580
  47.7 1.1 copy-start.25
  47.7 1.1 copy-start.26
  52.2 14.2 %all-to-all-start.1 = ((bf16[16,32,256]{2,1,0:T(8,128)(2,1)}), bf16[16,32,256]{2,1,0:T(8,128)(2,1)}, u32[]{:S(2)}, u32[]{:S(2)}) async-start(bf16[16,32,256]{2,1,0:T(8,128)(2,1)} %copy.233), calls=%async_computation.1 | async-start | bytes 524288 | tf_op jit(solution)/shard_map/all_to_all | solution.py:63
  59.5 6.9 %copy-start.33 = (s32[4]{0:T(128)S(1)}, s32[4]{0:T(128)}, u32[]{:S(2)}) copy-start(s32[4]{0:T(128)} %copy-done.32) | copy-start | bytes 52
  68.4 1.1 copy-start.18
  68.4 1.1 copy-start.46
  71.4 3.4 %copy-start.28 = (bf16[1,32,128]{2,1,0:T(8,128)(2,1)S(1)}, bf16[1,32,128]{2,1,0:T(8,128)(2,1)}, u32[]{:S(2)}) copy-start(bf16[1,32,128]{2,1,0:T(8,128)(2,1)} %copy-done.27) | copy-start | bytes 24580
  71.4 3.4 %copy-start.30 = (bf16[1,32,128]{2,1,0:T(8,128)(2,1)S(1)}, bf16[1,32,128]{2,1,0:T(8,128)(2,1)}, u32[]{:S(2)}) copy-start(bf16[1,32,128]{2,1,0:T(8,128)(2,1)} %copy-done.29) | copy-start | bytes 24580
  71.7 0.8 copy-start.3
  73.3 10.8 %collective-permute-start = (bf16[1024,128]{1,0:T(8,128)(2,1)}, bf16[1024,128]{1,0:T(8,128)(2,1)}, u32[]{:S(2)}, u32[]{:S(2)}) collective-permute-start(bf16[1024,128]{1,0:T(8,128)(2,1)} %bitcast_convert_fusion), channel_id=1, source_target_pairs={{0,1},{1,0},{2,3},{3,2},{4,5},{5,4},{6,7},{7,6},{8,9},{9,8},{10,11... | collective-permute-start | bytes 786440 | tf_op jit(solution)/shard_map/ppermute | solution.py:95
  77.2 2.9 copy-start.2
  80.1 1.5 copy-start.9
  81.6 1.5 copy-start.6
  83.1 1.2 copy-start.4
  83.1 1.4 slice-start
  86.3 1.1 copy-start.35
  86.4 5.9 %copy-start.19 = (bf16[9,128,256]{2,1,0:T(8,128)(2,1)S(1)}, bf16[9,128,256]{2,1,0:T(8,128)(2,1)}, u32[]{:S(2)}) copy-start(bf16[9,128,256]{2,1,0:T(8,128)(2,1)} %param.13) | copy-start | bytes 1769476
  88.5 11.4 %all-to-all-start.2 = ((bf16[16,32,128]{2,1,0:T(8,128)(2,1)}), bf16[16,32,128]{2,1,0:T(8,128)(2,1)S(1)}, u32[]{:S(2)}, u32[]{:S(2)}) async-start(bf16[16,32,128]{2,1,0:T(8,128)(2,1)} %copy.246), calls=%async_computation.2 | async-start | bytes 262144 | tf_op jit(solution)/shard_map/all_to_all | solution.py:63
  92.0 116.5 %all-gather.4.cloned.1.call-start = ((), (), s32[]{:S(2)}) async-start(), calls=%async_computation.4 | async-start | bytes 20123648 | tf_op jit(solution)/shard_map/all_gather | solution.py:169
  94.2 6.0 %copy-start.36 = (s32[4,3]{1,0:T(4,128)S(1)}, s32[4,3]{1,0:T(4,128)}, u32[]{:S(2)}) copy-start(s32[4,3]{1,0:T(4,128)} %broadcast_select_fusion.3) | copy-start | bytes 148
  95.7 5.2 %copy-start.41 = (pred[32]{0:T(512)(128)(4,1)S(1)}, pred[32]{0:T(512)(128)(4,1)}, u32[]{:S(2)}) copy-start(pred[32]{0:T(512)(128)(4,1)} %get-tuple-element.65) | copy-start | bytes 100
  95.7 5.3 %copy-start.42 = (pred[32]{0:T(512)(128)(4,1)S(1)}, pred[32]{0:T(512)(128)(4,1)}, u32[]{:S(2)}) copy-start(pred[32]{0:T(512)(128)(4,1)} %get-tuple-element.66) | copy-start | bytes 100
  99.9 1.3 copy-start.5
  101.2 3.5 %copy-start.14 = (bf16[32,32,128]{2,1,0:T(8,128)(2,1)S(1)}, bf16[32,32,128]{2,1,0:T(8,128)(2,1)}, u32[]{:S(2)}) copy-start(bf16[32,32,128]{2,1,0:T(8,128)(2,1)} %get-tuple-element.33) | copy-start | bytes 786436
  104.3 1.0 copy-start.11
  104.4 1.3 copy-start.17
  104.7 1.3 copy-start.13
  105.6 1.1 copy-start.16
  106.0 1.1 copy-start.12
  106.4 1.1 copy-start.10
  106.7 1.1 copy-start.15
  108.1 1.0 copy-start.8
  112.4 193.9 %all-reduce.9.cloned.1.call-start = ((), (), s32[]{:S(2)}) async-start(), calls=%async_computation.3 | async-start | bytes 2359296 | tf_op jit(solution)/shard_map/psum | solution.py:167
  113.5 0.7 copy-start.21
  113.5 0.7 copy-start.23
  215.9 92.7 %copy-start.1 = (bf16[9,256,128]{2,1,0:T(8,128)(2,1)S(1)}, bf16[9,256,128]{2,1,0:T(8,128)(2,1)}, u32[]{:S(2)}) copy-start(bf16[9,256,128]{2,1,0:T(8,128)(2,1)} %param.11) | copy-start | bytes 1769476
  (6 other events, 3.9 us)
Sparse Core Ops, SparseCore 0:
  112.5 95.9 all-gather.3
  212.5 93.6 all-reduce.8
